TPU v7x, 32 devices: a whole 2x2x4 slice. The times are simulated.
32 devices in a mesh: dp: 8 (over y, x, core), rep: 4 (over z).
Axes of the slice: x: 2, y: 2, z: 4, core: 2. Of those that a mesh axis runs over, the one named last changes fastest.
Arguments:
- tokens: bfloat16 [4096, 2048], P(('dp', 'rep')), may hold values from -6 to 6
- cotangent: bfloat16 [4096, 2048], P(('dp', 'rep')), may hold values from -0.125 to 0.125
- doc_ids: int32 [64, 64], P(('dp', 'rep')), may hold values from 0 to 3, never falling along the last dimension, each value on 1 to 32 neighbouring positions
- valid_len: int32 [64], P(('dp', 'rep')), may hold values from 16 to 64
- w_qkv: bfloat16 [2048, 384], P('dp'), may hold values from -0.125 to 0.125
- w_out: bfloat16 [2048, 128], P('dp'), may hold values from -0.5 to 0.5
- norm_gain: bfloat16 [2048], P('dp'), may hold values from 0.5 to 1.5
Outputs:
- grad_qkv: float32 [2048, 384], P('dp')
- grad_out: float32 [2048, 128], P('dp')
- grad_gain: float32 [2048], P('dp')
Inputs may be any that keep to these rules, and one draw needn't show every extreme that they name: `doc_ids`: within each row of 64 positions the ids never fall, and a document has 1 to 32 positions.
All inputs are finite; a program needn't handle non-finite values.
Results may differ from a plain program's by a relative error of at most 0.0079.
Values may be sent and summed in bfloat16 or wider, within the bound.
A program may use at most 64 MiB of HBM per device.

v0:
```python
import math
import jax
import jax.numpy as jnp
from jax import lax
from jax.sharding import PartitionSpec as P

NORM_EPS = 1e-06
ROPE_BASE = 1000000.0


def rotate(vector):
    half_size = vector.shape[-1] // 2
    return jnp.concatenate([-vector[..., half_size:], vector[..., :half_size]], axis=-1)


def unrotate(vector):
    half_size = vector.shape[-1] // 2
    return jnp.concatenate([vector[..., half_size:], -vector[..., :half_size]], axis=-1)


def tables(doc_rows, head_size):
    seq_length = doc_rows.shape[1]
    earlier = jnp.sum((doc_rows[:, None, :] < doc_rows[:, :, None]).astype(jnp.int32), axis=2)
    offsets = (jnp.arange(seq_length, dtype=jnp.int32)[None, :] - earlier).astype(jnp.float32)
    frequency = ROPE_BASE ** (-2.0 * jnp.arange(head_size // 2, dtype=jnp.float32) / head_size)
    angles = offsets[:, :, None] * frequency
    angles = jnp.concatenate([angles, angles], axis=2)
    return (jnp.cos(angles), jnp.sin(angles))


def forward_pass(inputs, doc_rows, w_qkv_full, gain_full):
    batches, seq_length, model_width = inputs.shape
    head_size = w_qkv_full.shape[1] // 3
    scale = 1.0 / math.sqrt(head_size)
    wide_in = inputs.astype(jnp.float32)
    inverse_rms = lax.rsqrt(jnp.mean(wide_in * wide_in, axis=2, keepdims=True) + NORM_EPS)
    scaled_in = wide_in * inverse_rms
    normed = (scaled_in * gain_full.astype(jnp.float32)).astype(jnp.bfloat16)
    projected = jnp.dot(
        normed.reshape(-1, model_width), w_qkv_full, preferred_element_type=jnp.float32
    )
    projected = projected.reshape(batches, seq_length, 3 * head_size)
    cosine, sine_part = tables(doc_rows, head_size)
    queries = projected[:, :, :head_size]
    keys_raw = projected[:, :, head_size : 2 * head_size]
    values_raw = projected[:, :, 2 * head_size :]
    query_rot = ((queries * cosine + rotate(queries) * sine_part) * scale).astype(jnp.bfloat16)
    key_rot = (keys_raw * cosine + rotate(keys_raw) * sine_part).astype(jnp.bfloat16)
    values = values_raw.astype(jnp.bfloat16)
    scores = jnp.einsum("msh,mth->mst", query_rot, key_rot, preferred_element_type=jnp.float32)
    order_row = jnp.arange(seq_length, dtype=jnp.int32)[:, None]
    order_col = jnp.arange(seq_length, dtype=jnp.int32)[None, :]
    allowed = (doc_rows[:, :, None] == doc_rows[:, None, :]) & (order_col <= order_row)[None]
    raised = jnp.where(allowed, jnp.exp(scores), 0.0)
    probabilities = raised / jnp.sum(raised, axis=2, keepdims=True)
    probs_low = probabilities.astype(jnp.bfloat16)
    attended = jnp.einsum(
        "mst,mth->msh", probs_low, values, preferred_element_type=jnp.float32
    ).astype(jnp.bfloat16)
    return (
        scaled_in,
        normed,
        query_rot,
        key_rot,
        values,
        probabilities,
        probs_low,
        attended,
        cosine,
        sine_part,
    )


def backward_pass(saved, live_dy, w_qkv_full, w_out_full):
    (
        scaled_in,
        normed,
        query_rot,
        key_rot,
        values,
        probabilities,
        probs_low,
        attended,
        cosine,
        sine_part,
    ) = saved
    batches, seq_length, model_width = live_dy.shape
    head_size = w_out_full.shape[1]
    scale = 1.0 / math.sqrt(head_size)
    d_attended = jnp.dot(
        live_dy.reshape(-1, model_width), w_out_full, preferred_element_type=jnp.float32
    )
    d_attended = d_attended.reshape(batches, seq_length, head_size).astype(jnp.bfloat16)
    d_probs = jnp.einsum("msh,mth->mst", d_attended, values, preferred_element_type=jnp.float32)
    d_values = jnp.einsum("mst,msh->mth", probs_low, d_attended, preferred_element_type=jnp.float32)
    d_scores = (
        probabilities * (d_probs - jnp.sum(probabilities * d_probs, axis=2, keepdims=True))
    ).astype(jnp.bfloat16)
    d_query = (
        jnp.einsum("mst,mth->msh", d_scores, key_rot, preferred_element_type=jnp.float32) * scale
    )
    d_key = jnp.einsum("mst,msh->mth", d_scores, query_rot, preferred_element_type=jnp.float32)
    d_query = d_query * cosine + unrotate(d_query * sine_part)
    d_key = d_key * cosine + unrotate(d_key * sine_part)
    d_qkv = jnp.concatenate([d_query, d_key, d_values], axis=2).astype(jnp.bfloat16)
    d_normed = lax.dot_general(
        d_qkv.reshape(-1, 3 * head_size),
        w_qkv_full,
        (((1,), (1,)), ((), ())),
        preferred_element_type=jnp.float32,
    )
    gain_term = jnp.sum(d_normed * scaled_in.reshape(-1, model_width), axis=0)
    return (d_qkv, gain_term)


def shards(tokens, cotangent, doc_ids, valid_len, w_qkv, w_out, norm_gain):
    batches, seq_length = doc_ids.shape
    model_width = tokens.shape[1]
    inputs = tokens.reshape(batches, seq_length, model_width)
    live_rows = jnp.arange(seq_length, dtype=jnp.int32)[None, :] < valid_len[:, None]
    live_dy = jnp.where(
        live_rows[:, :, None],
        cotangent.reshape(batches, seq_length, model_width),
        jnp.zeros((), jnp.bfloat16),
    )
    full_set = (
        lax.all_gather(w_qkv, "dp", axis=0, tiled=True),
        lax.all_gather(w_out, "dp", axis=0, tiled=True),
        lax.all_gather(norm_gain, "dp", axis=0, tiled=True),
    )
    saved = forward_pass(inputs, doc_ids, full_set[0], full_set[2])
    qkv_all, gain_total = backward_pass(saved, live_dy, full_set[0], full_set[1])
    normed_all = saved[1]
    attended_all = saved[7]
    head_size = w_out.shape[1]
    normed_flat = normed_all.reshape(-1, model_width)
    qkv_flat = qkv_all.reshape(-1, 3 * head_size)
    attended_flat = attended_all.reshape(-1, head_size)
    grad_qkv = lax.dot_general(
        normed_flat, qkv_flat, (((0,), (0,)), ((), ())), preferred_element_type=jnp.float32
    )
    grad_out = lax.dot_general(
        live_dy.reshape(-1, model_width),
        attended_flat,
        (((0,), (0,)), ((), ())),
        preferred_element_type=jnp.float32,
    )
    shares = (
        lax.psum_scatter(grad_qkv, "dp", scatter_dimension=0, tiled=True),
        lax.psum_scatter(grad_out, "dp", scatter_dimension=0, tiled=True),
    )
    shares = lax.psum((shares[0], shares[1]), "rep")
    gain_whole = lax.psum(gain_total, ("dp", "rep"))
    owned_rows = w_qkv.shape[0]
    gain_start = lax.axis_index("dp") * owned_rows
    gain_owned = lax.dynamic_slice_in_dim(gain_whole, gain_start, owned_rows, 0)
    replicas = lax.axis_size("rep")
    return (shares[0] / replicas, shares[1] / replicas, gain_owned / replicas)


def solution(mesh):
    in_specs = (
        P(("dp", "rep"), None),
        P(("dp", "rep"), None),
        P(("dp", "rep"), None),
        P(("dp", "rep")),
        P("dp", None),
        P("dp", None),
        P("dp"),
    )
    out_specs = (P("dp", None), P("dp", None), P("dp"))
    return jax.shard_map(shards, mesh=mesh, in_specs=in_specs, out_specs=out_specs, check_vma=False)
```

profile of v0, /device:TPU:0, one launch (start us, length us, event | category | flops | bytes accessed | tf_op | source)
XLA Modules:
  0.0 179.0 jit_solution(12147938299542766601)
XLA Ops:
  7.2 0.7 all-gather.3.cloned.1.call-update
  8.0 0.7 iota_compare_fusion.1
  8.8 1.3 multiply_reduce_fusion
  10.2 0.7 reshape.109
  10.8 10.4 %all-gather = bf16[8,1,256]{2,1,0:T(2,128)(2,1)S(1)} all-gather(bf16[1,1,256]{2,1,0:T(2,128)(2,1)S(1)} %reshape.109), channel_id=1, replica_groups=mesh['dp'=8,'rep'=4] {'dp'}, dimensions={0}, use_global_device_ids=true | all-gather | bytes 4608 | tf_op jit(solution)/shard_map/all_gather | solution.py:129
  21.3 0.8 convert_reduce_fusion
  22.1 9.8 %all_gather.11 = bf16[2048,128]{1,0:T(8,128)(2,1)S(1)} all-gather(bf16[256,128]{1,0:T(8,128)(2,1)} %param.12), channel_id=1, replica_groups=mesh['dp'=8,'rep'=4] {'dp'}, dimensions={0}, use_global_device_ids=true | all-gather | bytes 589824 | tf_op jit(solution)/shard_map/all_gather | solution.py:128
  32.2 0.3 convolution_convert_fusion.2
  32.7 5.5 %all-gather.3.cloned.1.call-done = bf16[2048,384]{1,0:T(8,128)(2,1)} async-done(((bf16[256,384]{1,0:T(8,128)(2,1)}), bf16[2048,384]{1,0:T(8,128)(2,1)}) %all-gather.3.cloned.1.call-update) | async-done | bytes 1572880 | tf_op jit(solution)/shard_map/all_gather | solution.py:127
  38.2 1.9 %fusion = f32[2,64,384]{2,1,0:T(8,128)S(1)} fusion(bf16[2,64,2048]{2,1,0:T(8,128)(2,1)S(1)} %bitcast.33, bf16[2048,384]{1,0:T(8,128)(2,1)} %all-gather.3.cloned.1.call-done), kind=kOutput, calls=%fused_computation.3 | convolution fusion | flops 201326592 | bytes 2293760 | tf_op jit(solution)/shard_map/dot_general | solution.py:39
  40.3 0.3 fusion.21
  40.8 1.5 convolution_bitcast_fusion.1
  42.4 0.3 fusion.32
  42.8 0.3 fusion.25
  43.3 0.3 fusion.26
  43.7 2.3 %convolution_bitcast_fusion = f32[2048,384]{1,0:T(8,128)} fusion(f32[2048]{0:T(1024)S(1)} %bitcast.38, f32[2,64]{1,0:T(2,128)S(1)} %rsqrt.13, bf16[2,64,128]{2,1,0:T(8,128)(2,1)S(1)} %convolution_convert_fusion.1, bf16[2,64,128]{2,1,0:T(8,128)(2,1)S(1)} %fusion.26, bf16[2,64,128]{2,1,0:T(8,128)(2,1)S(1)} %get-tuple-element.11, ...), kind=kOutput, calls=%fused_computation | convolution fusion | flops 202670080 | bytes 3777024 | tf_op jit(solution)/shard_map/dot_general | solution.py:139
  46.1 32.4 %reduce-scatter.5.cloned.1.call-done = f32[256,128]{1,0:T(8,128)} async-done(((f32[2048,128]{1,0:T(8,128)}), f32[256,128]{1,0:T(8,128)}) %reduce-scatter.5.cloned.1.call-update) | async-done | bytes 131088 | tf_op jit(solution)/shard_map/reduce_scatter | solution.py:150
  78.5 49.5 %reduce-scatter.3.cloned.1.call-done = f32[256,384]{1,0:T(8,128)} async-done(((f32[2048,384]{1,0:T(8,128)}), f32[256,384]{1,0:T(8,128)}) %reduce-scatter.3.cloned.1.call-update) | async-done | bytes 393232 | tf_op jit(solution)/shard_map/reduce_scatter | solution.py:149
  128.0 0.6 fusion.2
  128.7 39.5 %psum.23 = f32[2048]{0:T(1024)S(1)} all-reduce(f32[2048]{0:T(1024)S(1)} %fusion.2), channel_id=1, replica_groups=mesh['dp'=8,'rep'=4] {'dp','rep'}, use_global_device_ids=true, to_apply=%region_9.10 | all-reduce | flops 2048 | bytes 16384 | tf_op jit(solution)/shard_map/psum | solution.py:153
  168.2 0.6 dynamic-slice_multiply_fusion
  168.8 0.4 all-reduce.3.cloned.1.call-done
  169.2 1.8 broadcast_multiply_fusion
  170.9 1.6 broadcast_multiply_fusion.1
  (32 shorter events, 1.5 us)
Async XLA Ops:
  7.2 24.9 %copy-start.1 = (bf16[128,2048]{1,0:T(8,128)(2,1)S(1)}, bf16[128,2048]{1,0:T(8,128)(2,1)}, u32[]{:S(2)}) copy-start(bf16[128,2048]{1,0:T(8,128)(2,1)} %param.8) | copy-start | bytes 1572868
  7.2 31.0 %all-gather.3.cloned.1.call-start = ((), (), s32[]{:S(2)}) async-start(), calls=%async_computation.2 | async-start | bytes 1769472 | tf_op jit(solution)/shard_map/all_gather | solution.py:127
  7.9 70.6 %reduce-scatter.5.cloned.1.call-start = ((), (), s32[]{:S(2)}) async-start(), calls=%async_computation.4 | async-start | bytes 1179648 | tf_op jit(solution)/shard_map/reduce_scatter | solution.py:150
  8.8 23.7 %copy-start = (bf16[128,2048]{1,0:T(8,128)(2,1)S(1)}, bf16[128,2048]{1,0:T(8,128)(2,1)}, u32[]{:S(2)}) copy-start(bf16[128,2048]{1,0:T(8,128)(2,1)} %param.7) | copy-start | bytes 1572868
  38.2 2.5 %copy-start.3 = (s32[2,64]{1,0:T(2,128)S(1)}, s32[2,64]{1,0:T(2,128)}, u32[]{:S(2)}) copy-start(s32[2,64]{1,0:T(2,128)} %param.9) | copy-start | bytes 1540
  42.4 85.6 %reduce-scatter.3.cloned.1.call-start = ((), (), s32[]{:S(2)}) async-start(), calls=%async_computation.3 | async-start | bytes 3538944 | tf_op jit(solution)/shard_map/reduce_scatter | solution.py:149
  46.0 82.0 %copy-start.2 = (bf16[2048,384]{1,0:T(8,128)(2,1)S(1)}, bf16[2048,384]{1,0:T(8,128)(2,1)}, u32[]{:S(2)}) copy-start(bf16[2048,384]{1,0:T(8,128)(2,1)} %all-gather.3.cloned.1.call-done) | copy-start | bytes 4718596
  46.1 123.1 %all-reduce.3.cloned.1.call-start = ((), (), s32[]{:S(2)}) async-start(), calls=%async_computation.5 | async-start | bytes 1048576 | tf_op jit(solution)/shard_map/psum | solution.py:152
Sparse Core Ops, SparseCore 0:
  9.9 28.2 all-gather.2
  42.5 35.9 reduce-scatter.4
  81.9 46.0 reduce-scatter.2
  130.3 38.8 all-reduce.2
where the time goes:
time: 179 us
  waiting for transfers between devices  88.5 us (49%)
  blocking collectives  59.7 us (33%)
  between operations  13.9 us (8%)
  other arithmetic  8.19 us (5%)
  matrix products  7.7 us (4%)
    reduce_scatter x1, waiting for transfers between devices, shards(): lax.psum_scatter(grad_qkv, 'dp', scatter_dimension=0, tiled=True)  49.5 us
    psum x1, blocking collectives, shards(): gain_whole = lax.psum(gain_total, ('dp', 'rep'))  39.5 us
    reduce_scatter x1, waiting for transfers between devices, shards(): lax.psum_scatter(grad_out, 'dp', scatter_dimension=0, tiled=True)  32.4 us
    all_gather x1, blocking collectives, shards(): lax.all_gather(norm_gain, 'dp', axis=0, tiled=True)  10.4 us
    all_gather x1, blocking collectives, shards(): lax.all_gather(w_out, 'dp', axis=0, tiled=True)  9.83 us
    all_gather x1, waiting for transfers between devices, shards(): lax.all_gather(w_qkv, 'dp', axis=0, tiled=True)  5.52 us
    div x3, other arithmetic, shards(): return (shares[0] / replicas, shares[1] / replicas, gain_owned / replicas)  3.97 us
  transfers between devices with their start and end apart: 4, of which 4 were waited for; matrix products, arithmetic and copies ran while one was open for 5% of the time, Pallas kernels for 0%

commit v1 on v0

--- a/solution.py
+++ b/solution.py
@@ -6,6 +6,27 @@
 
 NORM_EPS = 1e-06
 ROPE_BASE = 1000000.0
+
+
+def collect(array, axis, dim):
+    peers, mine, rows = (lax.axis_size(axis), lax.axis_index(axis), array.shape[dim])
+    right = [(i, (i + 1) % peers) for i in range(peers)]
+    downward = [(i, (i - 1) % peers) for i in range(peers)]
+    whole = jnp.zeros((*array.shape[:dim], peers * rows, *array.shape[dim + 1 :]), array.dtype)
+    whole = lax.dynamic_update_slice_in_dim(whole, array, mine * rows, axis=dim)
+    from_left = from_right = array
+    middle = peers // 2
+    for step in range(1, middle + 1):
+        from_left = lax.ppermute(from_left, axis, right)
+        whole = lax.dynamic_update_slice_in_dim(
+            whole, from_left, (mine - step) % peers * rows, axis=dim
+        )
+        if step < peers - middle:
+            from_right = lax.ppermute(from_right, axis, downward)
+            whole = lax.dynamic_update_slice_in_dim(
+                whole, from_right, (mine + step) % peers * rows, axis=dim
+            )
+    return whole
 
 
 def rotate(vector):
@@ -125,7 +146,7 @@
     )
     full_set = (
         lax.all_gather(w_qkv, "dp", axis=0, tiled=True),
-        lax.all_gather(w_out, "dp", axis=0, tiled=True),
+        collect(w_out, "dp", 0),
         lax.all_gather(norm_gain, "dp", axis=0, tiled=True),
     )
     saved = forward_pass(inputs, doc_ids, full_set[0], full_set[2])

time: 179 us -> 182 us (1.017)
  blocking collectives: 59.7 us -> 49.2 us
  starting transfers between devices: 0.16 us -> 8.99 us
  waiting for transfers between devices: 88.5 us -> 91.9 us
    ppermute x0 -> x7, waiting for transfers between devices: none -> 10.2 us  [the longest x4 10.2 us: collect(): from_left = lax.ppermute(from_left, axis, right)]
    all_gather x1 -> x0, blocking collectives: 9.83 us -> none  [shards(): lax.all_gather(w_out, 'dp', axis=0, tiled=True)]
    ppermute x0 -> x7, starting transfers between devices: none -> 8.83 us  [the longest x3 7.88 us: collect(): from_right = lax.ppermute(from_right, axis, downward)]
    all_gather x1, waiting for transfers between devices: 5.52 us -> 0.02 us  [shards(): lax.all_gather(w_qkv, 'dp', axis=0, tiled=True)]
  transfers between devices with their start and end apart: 4 -> 11, of which waited for: 4 -> 6; matrix products, arithmetic and copies ran while one was open for 5% -> 6% of each run, Pallas kernels for 0% -> 0%
where the time goes in v1:
time: 182 us
  waiting for transfers between devices  91.9 us (50%)
  blocking collectives  49.2 us (27%)
  between operations  14.1 us (8%)
  starting transfers between devices  8.99 us (5%)
  other arithmetic  8.12 us (4%)
  matrix products  7.68 us (4%)
  local copies, waits for them, and re-layouts  1.9 us (1%)
    reduce_scatter x1, waiting for transfers between devices, shards(): lax.psum_scatter(grad_qkv, 'dp', scatter_dimension=0, tiled=True)  49.5 us
    psum x1, blocking collectives, shards(): gain_whole = lax.psum(gain_total, ('dp', 'rep'))  39.6 us
    reduce_scatter x1, waiting for transfers between devices, shards(): lax.psum_scatter(grad_out, 'dp', scatter_dimension=0, tiled=True)  31.8 us
    ppermute x4, waiting for transfers between devices, collect(): from_left = lax.ppermute(from_left, axis, right)  10.2 us
    all_gather x1, blocking collectives, shards(): lax.all_gather(norm_gain, 'dp', axis=0, tiled=True)  9.62 us
    ppermute x3, starting transfers between devices, collect(): from_right = lax.ppermute(from_right, axis, downward)  7.88 us
    div x3, other arithmetic, shards(): return (shares[0] / replicas, shares[1] / replicas, gain_owned / replicas)  3.97 us
  transfers between devices with their start and end apart: 11, of which 6 were waited for; matrix products, arithmetic and copies ran while one was open for 6% of the time, Pallas kernels for 0%

profile of v1, /device:TPU:0, one launch (start us, length us, event | category | flops | bytes accessed | tf_op | source)
XLA Modules:
  0.0 181.9 jit_solution(16544490035922999297)
XLA Ops:
  7.2 0.5 collective-permute-start
  7.8 2.9 %collective-permute-start.1 = (bf16[256,128]{1,0:T(8,128)(2,1)}, bf16[256,128]{1,0:T(8,128)(2,1)S(1)}, u32[]{:S(2)}, u32[]{:S(2)}) collective-permute-start(bf16[256,128]{1,0:T(8,128)(2,1)} %param.12), channel_id=1, source_target_pairs={{0,28},{4,0},{8,4},{12,8},{16,12},{20,16},{24,20},{28,24},{1,29},{... | collective-permute-start | bytes 196616 | tf_op jit(solution)/shard_map/ppermute | solution.py:25
  10.9 0.7 iota_compare_fusion.1
  11.7 1.2 multiply_reduce_fusion
  13.0 0.7 reshape.109
  13.6 9.6 %all-gather = bf16[8,1,256]{2,1,0:T(2,128)(2,1)S(1)} all-gather(bf16[1,1,256]{2,1,0:T(2,128)(2,1)S(1)} %reshape.109), channel_id=1, replica_groups=mesh['dp'=8,'rep'=4] {'dp'}, dimensions={0}, use_global_device_ids=true | all-gather | bytes 4608 | tf_op jit(solution)/shard_map/all_gather | solution.py:150
  23.3 0.8 convert_reduce_fusion
  24.3 0.9 constant_dynamic-update-slice_fusion.7
  25.6 0.4 collective-permute-start.2
  26.0 2.3 %collective-permute-start.3 = (bf16[256,128]{1,0:T(8,128)(2,1)S(1)}, bf16[256,128]{1,0:T(8,128)(2,1)S(1)}, u32[]{:S(2)}, u32[]{:S(2)}) collective-permute-start(bf16[256,128]{1,0:T(8,128)(2,1)S(1)} %collective-permute-done.1), channel_id=1, source_target_pairs={{0,28},{4,0},{8,4},{12,8},{16,12},{20,16},{24,20},{28,24},{1,29},{... | collective-permute-start | bytes 196616 | tf_op jit(solution)/shard_map/ppermute | solution.py:25
  28.3 1.9 %collective-permute-done.2 = bf16[256,128]{1,0:T(8,128)(2,1)S(1)} collective-permute-done((bf16[256,128]{1,0:T(8,128)(2,1)S(1)}, bf16[256,128]{1,0:T(8,128)(2,1)S(1)}, u32[]{:S(2)}, u32[]{:S(2)}) %collective-permute-start.2) | collective-permute-done | bytes 65568 | tf_op jit(solution)/shard_map/ppermute | solution.py:20
  30.2 2.6 %collective-permute-start.5 = (bf16[256,128]{1,0:T(8,128)(2,1)S(1)}, bf16[256,128]{1,0:T(8,128)(2,1)S(1)}, u32[]{:S(2)}, u32[]{:S(2)}) collective-permute-start(bf16[256,128]{1,0:T(8,128)(2,1)S(1)} %collective-permute-done.3), channel_id=1, source_target_pairs={{0,28},{4,0},{8,4},{12,8},{16,12},{20,16},{24,20},{28,24},{1,29},{... | collective-permute-start | bytes 196616 | tf_op jit(solution)/shard_map/ppermute | solution.py:25
  32.9 3.8 %collective-permute-done.4 = bf16[256,128]{1,0:T(8,128)(2,1)S(1)} collective-permute-done((bf16[256,128]{1,0:T(8,128)(2,1)S(1)}, bf16[256,128]{1,0:T(8,128)(2,1)S(1)}, u32[]{:S(2)}, u32[]{:S(2)}) %collective-permute-start.4) | collective-permute-done | bytes 65568 | tf_op jit(solution)/shard_map/ppermute | solution.py:20
  36.7 4.5 %collective-permute-done.6 = bf16[256,128]{1,0:T(8,128)(2,1)S(1)} collective-permute-done((bf16[256,128]{1,0:T(8,128)(2,1)S(1)}, bf16[256,128]{1,0:T(8,128)(2,1)S(1)}, u32[]{:S(2)}, u32[]{:S(2)}) %collective-permute-start.6) | collective-permute-done | bytes 65568 | tf_op jit(solution)/shard_map/ppermute | solution.py:20
  41.6 1.8 %fusion = f32[2,64,384]{2,1,0:T(8,128)S(1)} fusion(bf16[2,64,2048]{2,1,0:T(8,128)(2,1)S(1)} %bitcast.33, bf16[2048,384]{1,0:T(8,128)(2,1)} %all-gather.3.cloned.1.call-done), kind=kOutput, calls=%fused_computation.3 | convolution fusion | flops 201326592 | bytes 2293760 | tf_op jit(solution)/shard_map/dot_general | solution.py:60
  44.3 1.5 convolution_bitcast_fusion.1
  47.1 2.3 %convolution_bitcast_fusion = f32[2048,384]{1,0:T(8,128)} fusion(f32[2048]{0:T(1024)S(1)} %bitcast.38, f32[2,64]{1,0:T(2,128)S(1)} %rsqrt.13, bf16[2,64,128]{2,1,0:T(8,128)(2,1)S(1)} %convolution_convert_fusion.1, bf16[2,64,128]{2,1,0:T(8,128)(2,1)S(1)} %fusion.26, bf16[2,64,128]{2,1,0:T(8,128)(2,1)S(1)} %get-tuple-element.11, ...), kind=kOutput, calls=%fused_computation | convolution fusion | flops 202670080 | bytes 3777024 | tf_op jit(solution)/shard_map/dot_general | solution.py:160
  49.5 31.8 %reduce-scatter.5.cloned.1.call-done = f32[256,128]{1,0:T(8,128)} async-done(((f32[2048,128]{1,0:T(8,128)}), f32[256,128]{1,0:T(8,128)}) %reduce-scatter.5.cloned.1.call-update) | async-done | bytes 131088 | tf_op jit(solution)/shard_map/reduce_scatter | solution.py:171
  81.4 49.5 %reduce-scatter.3.cloned.1.call-done = f32[256,384]{1,0:T(8,128)} async-done(((f32[2048,384]{1,0:T(8,128)}), f32[256,384]{1,0:T(8,128)}) %reduce-scatter.3.cloned.1.call-update) | async-done | bytes 393232 | tf_op jit(solution)/shard_map/reduce_scatter | solution.py:170
  130.9 0.6 fusion.2
  131.5 39.6 %psum.23 = f32[2048]{0:T(1024)S(1)} all-reduce(f32[2048]{0:T(1024)S(1)} %fusion.2), channel_id=1, replica_groups=mesh['dp'=8,'rep'=4] {'dp','rep'}, use_global_device_ids=true, to_apply=%region_9.10 | all-reduce | flops 2048 | bytes 16384 | tf_op jit(solution)/shard_map/psum | solution.py:174
  171.1 0.6 dynamic-slice_multiply_fusion
  172.0 1.8 broadcast_multiply_fusion
  173.8 1.6 broadcast_multiply_fusion.1
  (54 shorter events, 3.7 us)
Async XLA Ops:
  7.2 18.2 %copy-start = (bf16[128,2048]{1,0:T(8,128)(2,1)S(1)}, bf16[128,2048]{1,0:T(8,128)(2,1)}, u32[]{:S(2)}) copy-start(bf16[128,2048]{1,0:T(8,128)(2,1)} %param.7) | copy-start | bytes 1572868
  7.2 18.1 %copy-start.1 = (bf16[128,2048]{1,0:T(8,128)(2,1)S(1)}, bf16[128,2048]{1,0:T(8,128)(2,1)}, u32[]{:S(2)}) copy-start(bf16[128,2048]{1,0:T(8,128)(2,1)} %param.8) | copy-start | bytes 1572868
  7.2 34.4 %all-gather.3.cloned.1.call-start = ((), (), s32[]{:S(2)}) async-start(), calls=%async_computation.2 | async-start | bytes 1769472 | tf_op jit(solution)/shard_map/all_gather | solution.py:148
  7.2 18.4 %collective-permute-start = (bf16[256,128]{1,0:T(8,128)(2,1)}, bf16[256,128]{1,0:T(8,128)(2,1)S(1)}, u32[]{:S(2)}, u32[]{:S(2)}) collective-permute-start(bf16[256,128]{1,0:T(8,128)(2,1)} %param.12), channel_id=1, source_target_pairs={{0,4},{4,8},{8,12},{12,16},{16,20},{20,24},{24,28},{28,0},{1,5},{5... | collective-permute-start | bytes 196616 | tf_op jit(solution)/shard_map/ppermute | solution.py:20
  7.8 18.2 %collective-permute-start.1 = (bf16[256,128]{1,0:T(8,128)(2,1)}, bf16[256,128]{1,0:T(8,128)(2,1)S(1)}, u32[]{:S(2)}, u32[]{:S(2)}) collective-permute-start(bf16[256,128]{1,0:T(8,128)(2,1)} %param.12), channel_id=1, source_target_pairs={{0,28},{4,0},{8,4},{12,8},{16,12},{20,16},{24,20},{28,24},{1,29},{... | collective-permute-start | bytes 196616 | tf_op jit(solution)/shard_map/ppermute | solution.py:25
  10.7 70.6 %reduce-scatter.5.cloned.1.call-start = ((), (), s32[]{:S(2)}) async-start(), calls=%async_computation.4 | async-start | bytes 1179648 | tf_op jit(solution)/shard_map/reduce_scatter | solution.py:171
  25.6 4.6 %collective-permute-start.2 = (bf16[256,128]{1,0:T(8,128)(2,1)S(1)}, bf16[256,128]{1,0:T(8,128)(2,1)S(1)}, u32[]{:S(2)}, u32[]{:S(2)}) collective-permute-start(bf16[256,128]{1,0:T(8,128)(2,1)S(1)} %collective-permute-done), channel_id=1, source_target_pairs={{0,4},{4,8},{8,12},{12,16},{16,20},{20,24},{24,28},{28,0},{1,5},{5... | collective-permute-start | bytes 196616 | tf_op jit(solution)/shard_map/ppermute | solution.py:20
  26.0 4.2 %collective-permute-start.3 = (bf16[256,128]{1,0:T(8,128)(2,1)S(1)}, bf16[256,128]{1,0:T(8,128)(2,1)S(1)}, u32[]{:S(2)}, u32[]{:S(2)}) collective-permute-start(bf16[256,128]{1,0:T(8,128)(2,1)S(1)} %collective-permute-done.1), channel_id=1, source_target_pairs={{0,28},{4,0},{8,4},{12,8},{16,12},{20,16},{24,20},{28,24},{1,29},{... | collective-permute-start | bytes 196616 | tf_op jit(solution)/shard_map/ppermute | solution.py:25
  30.2 6.5 %collective-permute-start.4 = (bf16[256,128]{1,0:T(8,128)(2,1)S(1)}, bf16[256,128]{1,0:T(8,128)(2,1)S(1)}, u32[]{:S(2)}, u32[]{:S(2)}) collective-permute-start(bf16[256,128]{1,0:T(8,128)(2,1)S(1)} %collective-permute-done.2), channel_id=1, source_target_pairs={{0,4},{4,8},{8,12},{12,16},{16,20},{20,24},{24,28},{28,0},{1,5},{5... | collective-permute-start | bytes 196616 | tf_op jit(solution)/shard_map/ppermute | solution.py:20
  30.2 6.5 %collective-permute-start.5 = (bf16[256,128]{1,0:T(8,128)(2,1)S(1)}, bf16[256,128]{1,0:T(8,128)(2,1)S(1)}, u32[]{:S(2)}, u32[]{:S(2)}) collective-permute-start(bf16[256,128]{1,0:T(8,128)(2,1)S(1)} %collective-permute-done.3), channel_id=1, source_target_pairs={{0,28},{4,0},{8,4},{12,8},{16,12},{20,16},{24,20},{28,24},{1,29},{... | collective-permute-start | bytes 196616 | tf_op jit(solution)/shard_map/ppermute | solution.py:25
  36.7 4.6 %collective-permute-start.6 = (bf16[256,128]{1,0:T(8,128)(2,1)S(1)}, bf16[256,128]{1,0:T(8,128)(2,1)S(1)}, u32[]{:S(2)}, u32[]{:S(2)}) collective-permute-start(bf16[256,128]{1,0:T(8,128)(2,1)S(1)} %collective-permute-done.4), channel_id=1, source_target_pairs={{0,4},{4,8},{8,12},{12,16},{16,20},{20,24},{24,28},{28,0},{1,5},{5... | collective-permute-start | bytes 196616 | tf_op jit(solution)/shard_map/ppermute | solution.py:20
  41.6 2.5 %copy-start.3 = (s32[2,64]{1,0:T(2,128)S(1)}, s32[2,64]{1,0:T(2,128)}, u32[]{:S(2)}) copy-start(s32[2,64]{1,0:T(2,128)} %param.9) | copy-start | bytes 1540
  45.8 85.1 %reduce-scatter.3.cloned.1.call-start = ((), (), s32[]{:S(2)}) async-start(), calls=%async_computation.3 | async-start | bytes 3538944 | tf_op jit(solution)/shard_map/reduce_scatter | solution.py:170
  49.5 81.4 %copy-start.2 = (bf16[2048,384]{1,0:T(8,128)(2,1)S(1)}, bf16[2048,384]{1,0:T(8,128)(2,1)}, u32[]{:S(2)}) copy-start(bf16[2048,384]{1,0:T(8,128)(2,1)} %all-gather.3.cloned.1.call-done) | copy-start | bytes 4718596
  49.5 122.6 %all-reduce.3.cloned.1.call-start = ((), (), s32[]{:S(2)}) async-start(), calls=%async_computation.5 | async-start | bytes 1048576 | tf_op jit(solution)/shard_map/psum | solution.py:173
Sparse Core Ops, SparseCore 0:
  10.9 28.6 all-gather.2
  45.9 35.4 reduce-scatter.4
  84.8 46.0 reduce-scatter.2
  133.1 38.8 all-reduce.2
